TPU v7x, 32 devices: a whole 2x2x4 slice. The times are simulated.
32 devices in a mesh: dp: 2 (over y), expert: 16 (over z, x, core).
Axes of the slice: x: 2, y: 2, z: 4, core: 2. Of those that a mesh axis runs over, the one named last changes fastest.
Arguments:
- grad_out: bfloat16 [4096, 4096], P(('dp', 'expert')), may hold values from -6 to 6
- saved_pre: bfloat16 [4096, 2, 1536], P(('dp', 'expert')), may hold values from -6 to 6
- gate_weight: bfloat16 [4096, 2], P(('dp', 'expert')), may hold values from 0.049804688 to 0.59765625
- routes: int32 [4096, 2], P(('dp', 'expert')), may hold values from 0 to 15, all different within a row; in each aligned block of 128 rows (0 to 127, 128 to 255, ...) at most 20 rows name the same one
- w_down: bfloat16 [16, 768, 4096], P('expert', None, 'dp'), may hold values from -0.09375 to 0.09375
Outputs:
- grad_pre: bfloat16 [4096, 2, 1536], P(('dp', 'expert'))
- grad_gate: bfloat16 [4096, 2], P(('dp', 'expert'))
- grad_down: bfloat16 [16, 768, 4096], P('expert', None, 'dp')
Inputs may be any that keep to these rules, and one draw needn't show every extreme that they name: Among the routes of one device's 128 tokens no expert is named more than 20 times, a bound that some block reaches; a token names 2 different experts.
All inputs are finite; a program needn't handle non-finite values.
Results may differ from a plain program's by a relative error of at most 0.0085.
Values may be sent and summed in bfloat16 or wider, within the bound.
A program may use at most 128 MiB of HBM per device.

v0:
```python
import jax
import jax.numpy as jnp
from jax import lax
from jax.sharding import PartitionSpec as P


def slot_positions(routes_flat, experts, capacity):
    expert_ids = jnp.arange(experts, dtype=jnp.int32)
    onehot = (routes_flat[:, None] == expert_ids[None, :]).astype(jnp.int32)
    rank = jnp.sum((jnp.cumsum(onehot, axis=0) - 1) * onehot, axis=1)
    return routes_flat * capacity + rank


def swiglu_parts(saved, hidden):
    gate_pre = saved[..., :hidden].astype(jnp.float32)
    up_pre = saved[..., hidden:].astype(jnp.float32)
    return (gate_pre, up_pre, jax.nn.silu(gate_pre))


def swiglu_grads(saved, weights, contraction, hidden):
    gate_pre, up_pre, active = swiglu_parts(saved, hidden)
    plain = lax.optimization_barrier((active * up_pre).astype(jnp.bfloat16))
    gate_grad = jnp.sum(
        plain.astype(jnp.float32) * contraction.astype(jnp.float32), axis=-1
    ).astype(jnp.bfloat16)
    back = weights.astype(jnp.float32)[..., None] * contraction.astype(jnp.float32)
    sigma = jax.nn.sigmoid(gate_pre)
    grad_gate_pre = back * up_pre * sigma * (1.0 + gate_pre * (1.0 - sigma))
    grad_up_pre = back * active
    return (jnp.concatenate([grad_gate_pre, grad_up_pre], axis=-1).astype(jnp.bfloat16), gate_grad)


def scaled_hidden(saved, weights, hidden):
    gate_pre, up_pre, active = swiglu_parts(saved, hidden)
    return (weights.astype(jnp.float32)[..., None] * active * up_pre).astype(jnp.bfloat16)


def on_device(grad_out, saved_pre, gate_weight, routes, w_down):
    tokens_dev, top_count = routes.shape
    hidden = w_down.shape[1]
    width = grad_out.shape[1]
    experts = lax.axis_size("expert")
    capacity = 5 * tokens_dev * top_count // (4 * experts)
    slots = experts * capacity
    route_count = tokens_dev * top_count
    positions = slot_positions(routes.reshape(route_count), experts, capacity)
    owners = (
        jnp.zeros((slots,), jnp.int32)
        .at[positions]
        .set(jnp.arange(route_count, dtype=jnp.int32) + 1)
    )
    filled = owners > 0
    route_ids = jnp.maximum(owners - 1, 0)
    saved_flat = saved_pre.reshape(route_count, 2 * hidden)
    weight_flat = gate_weight.reshape(route_count)
    send_rows = jnp.where(
        filled[:, None], jnp.take(grad_out, route_ids // top_count, axis=0), 0
    ).reshape(experts, capacity, width)
    send_saved = jnp.where(filled[:, None], jnp.take(saved_flat, route_ids, axis=0), 0).reshape(
        experts, capacity, 2 * hidden
    )
    send_weight = jnp.where(filled, jnp.take(weight_flat, route_ids), 0).reshape(experts, capacity)
    weights_full = lax.all_gather(w_down[0], "dp", axis=1, tiled=True)
    rows = lax.all_to_all(send_rows, "expert", split_axis=0, concat_axis=0, tiled=True)
    saved = lax.all_to_all(send_saved, "expert", split_axis=0, concat_axis=0, tiled=True)
    weights = lax.all_to_all(send_weight, "expert", split_axis=0, concat_axis=0, tiled=True)
    flat_rows = rows.reshape(-1, width)
    product = lax.dot_general(
        flat_rows, weights_full, (((1,), (1,)), ((), ())), preferred_element_type=jnp.float32
    )
    contraction = product.astype(jnp.bfloat16).reshape(rows.shape[0], rows.shape[1], hidden)
    grads, gate_grad = swiglu_grads(saved, weights, contraction, hidden)
    scaled = scaled_hidden(saved, weights, hidden)
    back_grads = lax.all_to_all(grads, "expert", split_axis=0, concat_axis=0, tiled=True)
    back_gate = lax.all_to_all(gate_grad, "expert", split_axis=0, concat_axis=0, tiled=True)
    back_grads, back_gate, rows_in, scaled_in = (back_grads, back_gate, rows, scaled)
    grad_pre = jnp.take(back_grads.reshape(slots, 2 * hidden), positions, axis=0)
    grad_gate = jnp.take(back_gate.reshape(slots), positions)
    rows_flat = rows_in.reshape(slots, width)
    scaled_flat = scaled_in.reshape(slots, hidden)
    columns = lax.all_to_all(rows_flat, "dp", split_axis=1, concat_axis=0, tiled=True)
    grad_down = lax.dot_general(
        lax.all_gather(scaled_flat, "dp", axis=0, tiled=True),
        columns,
        (((0,), (0,)), ((), ())),
        preferred_element_type=jnp.float32,
    )
    return (
        grad_pre.reshape(tokens_dev, top_count, 2 * hidden),
        grad_gate.reshape(tokens_dev, top_count),
        grad_down.astype(jnp.bfloat16)[None],
    )


def solution(mesh):
    return jax.shard_map(
        on_device,
        mesh=mesh,
        in_specs=(
            P(("dp", "expert"), None),
            P(("dp", "expert"), None, None),
            P(("dp", "expert"), None),
            P(("dp", "expert"), None),
            P("expert", None, "dp"),
        ),
        out_specs=(
            P(("dp", "expert"), None, None),
            P(("dp", "expert"), None),
            P("expert", None, "dp"),
        ),
        check_vma=False,
    )
```

profile of v0, /device:TPU:1, one launch (start us, length us, event | category | flops | bytes accessed | tf_op | source)
XLA Modules:
  0.0 230.2 jit_solution(5722844208773332598)
XLA Ops:
  11.8 2.4 %gather_fusion = bf16[320]{0:T(512)(128)(2,1)S(1)} fusion(bf16[256]{0:T(256)(128)(2,1)S(1)} %reshape.156, s32[1024]{0:T(1024)S(1)} %pad_clamp_fusion.2), kind=kCustom, calls=%fused_computation | custom fusion | bytes 2560 | tf_op jit(solution)/shard_map/jit(_take)/gather | solution.py:62
  14.9 7.3 %all-to-all-start = ((bf16[16,1,20]{2,1,0:T(2,128)(2,1)}), bf16[16,1,20]{2,1,0:T(2,128)(2,1)S(1)}, u32[]{:S(2)}, u32[]{:S(2)}) async-start(bf16[16,1,20]{2,1,0:T(2,128)(2,1)} %all_to_all.43), calls=%async_computation | async-start | bytes 16384 | tf_op jit(solution)/shard_map/all_to_all | solution.py:66
  22.2 3.8 %gather_fusion.1 = bf16[320,4096]{1,0:T(8,128)(2,1)} fusion(bf16[128,4096]{1,0:T(8,128)(2,1)S(1)} %copy-done, s32[1024]{0:T(1024)S(1)} %pad_clamp_fusion.1), kind=kCustom, calls=%fused_computation.1 | custom fusion | bytes 5244160 | tf_op jit(solution)/shard_map/jit(_take)/gather | solution.py:57
  26.1 4.3 %gather.30 = bf16[16,20,4096]{2,1,0:T(8,128)(2,1)} reshape(bf16[320,4096]{1,0:T(8,128)(2,1)} %gather_fusion.1) | data formatting | bytes 5242880 | tf_op jit(solution)/shard_map/jit(_take)/gather | solution.py:57
  30.5 4.0 %select_select_fusion = bf16[16,20,4096]{2,1,0:T(8,128)(2,1)} fusion(bf16[16,20,4096]{2,1,0:T(8,128)(2,1)} %gather.30, pred[16,20]{1,0:T(8,128)(4,1)S(1)} %broadcast_in_dim.95, pred[16,20]{1,0:T(8,128)(4,1)S(1)} %broadcast_in_dim.93), kind=kLoop, calls=%fused_computation.9 | loop fusion | flops 2621440 | bytes 5243520 | tf_op jit(solution)/shard_map/jit(_where)/select_n | solution.py:56
  34.5 6.0 %all-to-all-start.1 = ((bf16[16,20,4096]{2,1,0:T(8,128)(2,1)}), bf16[16,20,4096]{2,1,0:T(8,128)(2,1)}, u32[]{:S(2)}, u32[]{:S(2)}) async-start(bf16[16,20,4096]{2,1,0:T(8,128)(2,1)} %select_select_fusion), calls=%async_computation.1 | async-start | bytes 6291456 | tf_op jit(solution)/shard_map/all_to_all | solution.py:64
  42.0 2.2 gather_fusion.2
  45.8 54.7 %all-to-all-done.1 = bf16[16,20,4096]{2,1,0:T(8,128)(2,1)} async-done(((bf16[16,20,4096]{2,1,0:T(8,128)(2,1)}), bf16[16,20,4096]{2,1,0:T(8,128)(2,1)}, u32[]{:S(2)}, u32[]{:S(2)}) %all-to-all-start.1) | async-done | bytes 2621472 | tf_op jit(solution)/shard_map/all_to_all | solution.py:64
  100.5 14.9 %all-to-all-start.2 = ((bf16[16,20,1536]{2,1,0:T(8,128)(2,1)}), bf16[16,20,1536]{2,1,0:T(8,128)(2,1)S(1)}, u32[]{:S(2)}, u32[]{:S(2)}) async-start(bf16[16,20,1536]{2,1,0:T(8,128)(2,1)} %select_select_fusion.1), calls=%async_computation.2 | async-start | bytes 2359296 | tf_op jit(solution)/shard_map/all_to_all | solution.py:65
  115.4 7.4 %all_to_all.39 = bf16[320,2,2048]{2,1,0:T(2,128)(2,1)} reshape(bf16[16,20,4096]{2,1,0:T(8,128)(2,1)} %all-to-all-done.1) | data formatting | bytes 5242880 | tf_op jit(solution)/shard_map/all_to_all | solution.py:81
  122.8 4.4 %copy.30 = bf16[320,2,2048]{2,0,1:T(8,128)(2,1)} copy(bf16[320,2,2048]{2,1,0:T(2,128)(2,1)} %all_to_all.39) | data formatting | bytes 5242880 | tf_op jit(solution)/shard_map/all_to_all | solution.py:81
  127.2 13.7 %all-to-all-done.2 = bf16[16,20,1536]{2,1,0:T(8,128)(2,1)S(1)} async-done(((bf16[16,20,1536]{2,1,0:T(8,128)(2,1)}), bf16[16,20,1536]{2,1,0:T(8,128)(2,1)S(1)}, u32[]{:S(2)}, u32[]{:S(2)}) %all-to-all-start.2) | async-done | bytes 983072 | tf_op jit(solution)/shard_map/all_to_all | solution.py:65
  140.9 5.2 %all-to-all-start.5 = ((bf16[320,2,2048]{2,0,1:T(8,128)(2,1)}), bf16[320,2,2048]{2,0,1:T(8,128)(2,1)}, u32[]{:S(2)}, u32[]{:S(2)}) async-start(bf16[320,2,2048]{2,0,1:T(8,128)(2,1)} %copy.30), calls=%async_computation.5 | async-start | bytes 5242880 | tf_op jit(solution)/shard_map/all_to_all | solution.py:81
  147.3 4.3 %reshape.157 = bf16[320,4096]{1,0:T(8,128)(2,1)} reshape(bf16[16,20,4096]{2,1,0:T(8,128)(2,1)} %all-to-all-done.1) | data formatting | bytes 5242880 | tf_op jit(solution)/shard_map/reshape | solution.py:67
  151.5 6.8 %fusion.6 = f32[320,768]{1,0:T(8,128)} fusion(bf16[320,4096]{1,0:T(8,128)(2,1)} %reshape.157, bf16[1,768,4096]{2,1,0:T(8,128)(2,1)} %all-gather.3.cloned.1.call-done), kind=kOutput, calls=%fused_computation.19 | convolution fusion | flops 2013757440 | bytes 9895936 | tf_op jit(solution)/shard_map/dot_general | solution.py:68
  159.6 3.2 %fusion.11 = (bf16[16,20,768]{2,1,0:T(8,128)(2,1)}, bf16[16,20,768]{2,1,0:T(8,128)(2,1)}, bf16[16,20,768]{2,1,0:T(8,128)(2,1)}, bf16[16,20]{1,0:T(8,128)(2,1)S(1)}) fusion(f32[16,20,768]{2,1,0:T(8,128)S(1)} %reshape.163, f32[16,20]{1,0:T(8,128)S(1)} %bitcast.36, bf16[16,20,1536]{2,1,0:T(8,128)(2,1)S(1)} %all-to-all-done.2, bf16[16,20,768]{2,1,0:T(8,128)(2,1)} %fusion.12), kind=kLoop, calls=%fused_computation.22 | loop fusion | flops 5406400 | bytes 3934080 | tf_op jit(solution)/shard_map/convert.2
  163.4 13.5 %all-to-all-done.5 = bf16[320,2,2048]{2,0,1:T(8,128)(2,1)} async-done(((bf16[320,2,2048]{2,0,1:T(8,128)(2,1)}), bf16[320,2,2048]{2,0,1:T(8,128)(2,1)}, u32[]{:S(2)}, u32[]{:S(2)}) %all-to-all-start.5) | async-done | bytes 2621472 | tf_op jit(solution)/shard_map/all_to_all | solution.py:81
  177.0 7.3 %all-to-all-start.4 = ((bf16[16,1,20]{2,1,0:T(2,128)(2,1)}), bf16[16,1,20]{2,1,0:T(2,128)(2,1)S(1)}, u32[]{:S(2)}, u32[]{:S(2)}) async-start(bf16[16,1,20]{2,1,0:T(2,128)(2,1)} %copy.29), calls=%async_computation.4 | async-start | bytes 16384 | tf_op jit(solution)/shard_map/all_to_all | solution.py:75
  184.2 2.4 %pad_maximum_fusion = bf16[16,20,1536]{2,1,0:T(8,128)(2,1)} fusion(bf16[16,20,768]{2,1,0:T(8,128)(2,1)} %get-tuple-element.20, bf16[16,20,768]{2,1,0:T(8,128)(2,1)} %get-tuple-element.19), kind=kLoop, calls=%fused_computation.29 | loop fusion | flops 1966080 | bytes 1966080 | tf_op jit(solution)/shard_map/concatenate | solution.py:30
  186.6 3.4 %all-to-all-done.4 = bf16[16,1,20]{2,1,0:T(2,128)(2,1)S(1)} async-done(((bf16[16,1,20]{2,1,0:T(2,128)(2,1)}), bf16[16,1,20]{2,1,0:T(2,128)(2,1)S(1)}, u32[]{:S(2)}, u32[]{:S(2)}) %all-to-all-start.4) | async-done | bytes 672 | tf_op jit(solution)/shard_map/all_to_all | solution.py:75
  190.0 4.2 %all-to-all-start.3 = ((bf16[16,20,1536]{2,1,0:T(8,128)(2,1)}), bf16[16,20,1536]{2,1,0:T(8,128)(2,1)S(1)}, u32[]{:S(2)}, u32[]{:S(2)}) async-start(bf16[16,20,1536]{2,1,0:T(8,128)(2,1)} %pad_maximum_fusion), calls=%async_computation.3 | async-start | bytes 2359296 | tf_op jit(solution)/shard_map/all_to_all | solution.py:74
  195.3 13.4 %all_gather.7 = bf16[640,768]{1,0:T(8,128)(2,1)S(1)} all-gather(bf16[320,768]{1,0:T(8,128)(2,1)} %reshape.161), channel_id=1, replica_groups=mesh['dp'=2,'expert'=16] {'dp'}, dimensions={0}, use_global_device_ids=true | all-gather | bytes 1474560 | tf_op jit(solution)/shard_map/all_gather | solution.py:83
  208.7 5.8 %fusion.2 = bf16[1,768,2048]{2,1,0:T(8,128)(2,1)} fusion(bf16[640,768]{1,0:T(8,128)(2,1)S(1)} %all_gather.7, bf16[640,2048]{1,0:T(8,128)(2,1)} %bitcast.7), kind=kOutput, calls=%fused_computation.10 | convolution fusion | flops 2014838784 | bytes 6750208 | tf_op jit(solution)/shard_map/dot_general | solution.py:82
  217.3 2.5 %all-to-all-done.3 = bf16[16,20,1536]{2,1,0:T(8,128)(2,1)S(1)} async-done(((bf16[16,20,1536]{2,1,0:T(8,128)(2,1)}), bf16[16,20,1536]{2,1,0:T(8,128)(2,1)S(1)}, u32[]{:S(2)}, u32[]{:S(2)}) %all-to-all-start.3) | async-done | bytes 983072 | tf_op jit(solution)/shard_map/all_to_all | solution.py:74
  (55 shorter events, 18.9 us)
Async XLA Ops:
  7.2 15.1 %copy-start = (bf16[128,4096]{1,0:T(8,128)(2,1)S(1)}, bf16[128,4096]{1,0:T(8,128)(2,1)}, u32[]{:S(2)}) copy-start(bf16[128,4096]{1,0:T(8,128)(2,1)} %param.5) | copy-start | bytes 3145732
  14.9 19.7 %all-to-all-start = ((bf16[16,1,20]{2,1,0:T(2,128)(2,1)}), bf16[16,1,20]{2,1,0:T(2,128)(2,1)S(1)}, u32[]{:S(2)}, u32[]{:S(2)}) async-start(bf16[16,1,20]{2,1,0:T(2,128)(2,1)} %all_to_all.43), calls=%async_computation | async-start | bytes 16384 | tf_op jit(solution)/shard_map/all_to_all | solution.py:66
  34.5 65.9 %all-to-all-start.1 = ((bf16[16,20,4096]{2,1,0:T(8,128)(2,1)}), bf16[16,20,4096]{2,1,0:T(8,128)(2,1)}, u32[]{:S(2)}, u32[]{:S(2)}) async-start(bf16[16,20,4096]{2,1,0:T(8,128)(2,1)} %select_select_fusion), calls=%async_computation.1 | async-start | bytes 6291456 | tf_op jit(solution)/shard_map/all_to_all | solution.py:64
  40.6 1.1 copy-start.2
  40.6 111.0 %all-gather.3.cloned.1.call-start = ((), (), s32[]{:S(2)}) async-start(), calls=%async_computation.6 | async-start | bytes 9437184 | tf_op jit(solution)/shard_map/all_gather | solution.py:63
  100.5 40.4 %all-to-all-start.2 = ((bf16[16,20,1536]{2,1,0:T(8,128)(2,1)}), bf16[16,20,1536]{2,1,0:T(8,128)(2,1)S(1)}, u32[]{:S(2)}, u32[]{:S(2)}) async-start(bf16[16,20,1536]{2,1,0:T(8,128)(2,1)} %select_select_fusion.1), calls=%async_computation.2 | async-start | bytes 2359296 | tf_op jit(solution)/shard_map/all_to_all | solution.py:65
  140.9 36.1 %all-to-all-start.5 = ((bf16[320,2,2048]{2,0,1:T(8,128)(2,1)}), bf16[320,2,2048]{2,0,1:T(8,128)(2,1)}, u32[]{:S(2)}, u32[]{:S(2)}) async-start(bf16[320,2,2048]{2,0,1:T(8,128)(2,1)} %copy.30), calls=%async_computation.5 | async-start | bytes 5242880 | tf_op jit(solution)/shard_map/all_to_all | solution.py:81
  177.0 13.1 %all-to-all-start.4 = ((bf16[16,1,20]{2,1,0:T(2,128)(2,1)}), bf16[16,1,20]{2,1,0:T(2,128)(2,1)S(1)}, u32[]{:S(2)}, u32[]{:S(2)}) async-start(bf16[16,1,20]{2,1,0:T(2,128)(2,1)} %copy.29), calls=%async_computation.4 | async-start | bytes 16384 | tf_op jit(solution)/shard_map/all_to_all | solution.py:75
  186.6 7.8 %copy-start.1 = (bf16[16,20,768]{2,1,0:T(8,128)(2,1)S(1)}, bf16[16,20,768]{2,1,0:T(8,128)(2,1)}, u32[]{:S(2)}) copy-start(bf16[16,20,768]{2,1,0:T(8,128)(2,1)} %get-tuple-element.21) | copy-start | bytes 1474564
  190.0 29.8 %all-to-all-start.3 = ((bf16[16,20,1536]{2,1,0:T(8,128)(2,1)}), bf16[16,20,1536]{2,1,0:T(8,128)(2,1)S(1)}, u32[]{:S(2)}, u32[]{:S(2)}) async-start(bf16[16,20,1536]{2,1,0:T(8,128)(2,1)} %pad_maximum_fusion), calls=%async_computation.3 | async-start | bytes 2359296 | tf_op jit(solution)/shard_map/all_to_all | solution.py:74
Sparse Core Ops, SparseCore 0:
  42.9 80.9 all-gather.2
where the time goes:
time: 233 us; the launch traced here: 230 us
  waiting for transfers between devices  88.5 us (38%)
  starting transfers between devices  44.9 us (19%)
  local copies, waits for them, and re-layouts  42 us (18%)
  other arithmetic  14.6 us (6%)
  between operations  14.3 us (6%)
  blocking collectives  13.4 us (6%)
  matrix products  12.5 us (5%)
    all_to_all x1, waiting for transfers between devices, on_device(): lax.all_to_all(send_rows, 'expert', split_axis=0, concat_axis=0, tiled=True)  54.7 us
    all_to_all x1, starting transfers between devices, on_device(): lax.all_to_all(send_saved, 'expert', split_axis=0, concat_axis=0, tiled=T...  14.9 us
    all_to_all x1, waiting for transfers between devices, on_device(): lax.all_to_all(send_saved, 'expert', split_axis=0, concat_axis=0, tiled=T...  13.7 us
    all_to_all x1, waiting for transfers between devices, on_device(): lax.all_to_all(rows_flat, 'dp', split_axis=1, concat_axis=0, tiled=True)  13.5 us
    all_gather x1, blocking collectives, on_device(): lax.all_gather(scaled_flat, 'dp', axis=0, tiled=True)  13.4 us
    all_to_all x2, local copies, waits for them, and re-layouts, on_device(): lax.all_to_all(rows_flat, 'dp', split_axis=1, concat_axis=0, tiled=True)  11.8 us
    gather x2, local copies, waits for them, and re-layouts, on_device(): jnp.take(grad_out, route_ids // top_count, axis=0)  8.1 us
    all_to_all x1, starting transfers between devices, on_device(): lax.all_to_all(send_weight, 'expert', split_axis=0, concat_axis=0, tiled=...  7.31 us
  transfers between devices with their start and end apart: 7, of which 5 were waited for; matrix products, arithmetic and copies ran while one was open for 22% of the time, Pallas kernels for 0%

commit v1 on v0

v1 whole, which is shorter than its diff:
```python
import jax
import jax.numpy as jnp
from jax import lax
from jax.sharding import PartitionSpec as P

BF16 = jnp.bfloat16
F32 = jnp.float32


def slot_positions(routes_flat, experts, capacity):
    expert_ids = jnp.arange(experts, dtype=jnp.int32)
    onehot = (routes_flat[:, None] == expert_ids[None, :]).astype(jnp.int32)
    rank = jnp.sum((jnp.cumsum(onehot, axis=0) - 1) * onehot, axis=1)
    return routes_flat * capacity + rank


def swiglu_parts(saved, hidden):
    gate_pre = saved[..., :hidden].astype(F32)
    up_pre = saved[..., hidden:].astype(F32)
    return (gate_pre, up_pre, jax.nn.silu(gate_pre))


def swiglu_grads(saved, weights, contraction, hidden):
    gate_pre, up_pre, active = swiglu_parts(saved, hidden)
    plain = (active * up_pre).astype(BF16)
    gate_grad = jnp.sum(plain.astype(F32) * contraction.astype(F32), axis=-1).astype(BF16)
    back = weights.astype(F32)[..., None] * contraction.astype(F32)
    sigma = jax.nn.sigmoid(gate_pre)
    grad_gate_pre = back * up_pre * sigma * (1.0 + gate_pre * (1.0 - sigma))
    grad_up_pre = back * active
    return (jnp.concatenate([grad_gate_pre, grad_up_pre], axis=-1).astype(BF16), gate_grad)


def scaled_hidden(saved, weights, hidden):
    gate_pre, up_pre, active = swiglu_parts(saved, hidden)
    return (weights.astype(F32)[..., None] * active * up_pre).astype(BF16)


def dot(a, b, dims):
    return lax.dot_general(a, b, (dims, ((), ())), preferred_element_type=F32)


def on_device(grad_out, saved_pre, gate_weight, routes, w_down):
    tokens_dev, top_count = routes.shape
    hidden = w_down.shape[1]
    half = w_down.shape[2]
    experts = lax.axis_size("expert")
    replicas = lax.axis_size("dp")
    capacity = 5 * tokens_dev * top_count // (4 * experts)
    slots = experts * capacity
    positions = slot_positions(routes.reshape(-1), experts, capacity).reshape(tokens_dev, top_count)
    slot_ids = jnp.arange(slots, dtype=jnp.int32)
    picks = [
        (positions[:, k][None, :] == slot_ids[:, None]).astype(BF16) for k in range(top_count)
    ]
    pick = sum(picks[1:], picks[0])
    devices = replicas * experts
    send_rows = jnp.stack(
        [
            dot(pick, grad_out[:, d * half : (d + 1) * half], ((1,), (0,))).astype(BF16)
            for d in range(replicas)
        ]
    ).reshape(devices, capacity, half)
    scaled = scaled_hidden(saved_pre, gate_weight, hidden)
    send_scaled = sum(dot(picks[k], scaled[:, k], ((1,), (0,))) for k in range(top_count))
    send_scaled = send_scaled.astype(BF16).reshape(experts, capacity, hidden)
    rows = lax.all_to_all(send_rows, ("dp", "expert"), split_axis=0, concat_axis=0, tiled=True)
    scaled_in = lax.all_to_all(send_scaled, "expert", split_axis=0, concat_axis=0, tiled=True)
    scaled_in = lax.all_gather(scaled_in.reshape(slots, hidden), "dp", axis=0, tiled=True)
    rows = rows.reshape(devices * capacity, half)
    partial = dot(rows, w_down[0], ((1,), (1,))).astype(BF16).reshape(devices, capacity, hidden)
    parts = lax.all_to_all(partial, ("dp", "expert"), split_axis=0, concat_axis=0, tiled=True)
    parts = parts.reshape(replicas, slots, hidden)
    contraction = jnp.stack(
        [
            sum(dot(picks[k], parts[d], ((0,), (0,))) for d in range(replicas))
            for k in range(top_count)
        ],
        axis=1,
    ).astype(BF16)
    grads, gate_grad = swiglu_grads(saved_pre, gate_weight, contraction, hidden)
    grad_down = dot(scaled_in, rows, ((0,), (0,))).astype(BF16)
    return grads, gate_grad, grad_down[None]


def solution(mesh):
    return jax.shard_map(
        on_device,
        mesh=mesh,
        in_specs=(
            P(("dp", "expert"), None),
            P(("dp", "expert"), None, None),
            P(("dp", "expert"), None),
            P(("dp", "expert"), None),
            P("expert", None, "dp"),
        ),
        out_specs=(
            P(("dp", "expert"), None, None),
            P(("dp", "expert"), None),
            P("expert", None, "dp"),
        ),
        check_vma=False,
    )
```

time: 233 us -> 201 us (0.86)
  blocking collectives: 13.4 us -> 91.8 us
  waiting for transfers between devices: 88.5 us -> 39.6 us
  starting transfers between devices: 44.9 us -> 8.91 us
  local copies, waits for them, and re-layouts: 42 us -> 28.3 us
  between operations: 14.3 us -> 0.74 us
  matrix products: 12.5 us -> 22.2 us
  other arithmetic: 14.6 us -> 7.29 us
    all_to_all x0 -> x1, blocking collectives: none -> 78.6 us  [on_device(): lax.all_to_all(send_rows, ('dp', 'expert'), split_axis=0, concat_axis=0,...]
    all_to_all x6 -> x2, waiting for transfers between devices: 87.9 us -> 39.6 us  [the longest x1 27 us: on_device(): lax.all_to_all(partial, ('dp', 'expert'), split_axis=0, concat_axis=0, ti...]
    all_to_all x6 -> x2, starting transfers between devices: 44.9 us -> 8.91 us  [the longest x1 5.01 us: on_device(): lax.all_to_all(send_scaled, 'expert', split_axis=0, concat_axis=0, tiled=...]
    gather x9 -> x0, local copies, waits for them, and re-layouts: 16.6 us -> none  [the longest x2 8.1 us: on_device(): jnp.take(grad_out, route_ids // top_count, axis=0)]
    all_to_all x3 -> x0, local copies, waits for them, and re-layouts: 12.5 us -> none  [the longest x2 11.8 us: on_device(): lax.all_to_all(rows_flat, 'dp', split_axis=1, concat_axis=0, tiled=True)]
    reshape x7 -> x5, local copies, waits for them, and re-layouts: 6.05 us -> 16.3 us  [the longest x1 5.18 us: on_device(): rows = rows.reshape(devices * capacity, half)]
    dot_general x2 -> x10, matrix products: 12.5 us -> 22.2 us  [dot(): return lax.dot_general(a, b, (dims, ((), ())), preferred_element_type=F32)]
    select_n x6 -> x0, other arithmetic: 7 us -> none  [the longest x1 4.02 us: on_device(): jnp.where(filled[:, None], jnp.take(grad_out, route_ids // top_count, axi...]
  transfers between devices with their start and end apart: 7 -> 2, of which waited for: 5 -> 2; matrix products, arithmetic and copies ran while one was open for 22% -> 3% of each run, Pallas kernels for 0% -> 0%
where the time goes in v1:
time: 201 us; the launch traced here: 199 us
  blocking collectives  91.8 us (46%)
  waiting for transfers between devices  39.6 us (20%)
  local copies, waits for them, and re-layouts  28.3 us (14%)
  matrix products  22.2 us (11%)
  starting transfers between devices  8.91 us (4%)
  other arithmetic  7.29 us (4%)
    all_to_all x1, blocking collectives, on_device(): lax.all_to_all(send_rows, ('dp', 'expert'), split_axis=0, concat_axis=0,...  78.6 us
    all_to_all x1, waiting for transfers between devices, on_device(): lax.all_to_all(partial, ('dp', 'expert'), split_axis=0, concat_axis=0, ti...  27 us
    dot_general x10, matrix products, dot(): return lax.dot_general(a, b, (dims, ((), ())), preferred_element_type=F32)  22.2 us
    all_gather x1, blocking collectives, on_device(): lax.all_gather(scaled_in.reshape(slots, hidden), 'dp', axis=0, tiled=True)  13.2 us
    all_to_all x1, waiting for transfers between devices, on_device(): lax.all_to_all(send_scaled, 'expert', split_axis=0, concat_axis=0, tiled=...  12.6 us
    reshape x1, local copies, waits for them, and re-layouts, on_device(): rows = rows.reshape(devices * capacity, half)  5.18 us
    reshape x1, local copies, waits for them, and re-layouts, on_device(): send_rows = jnp.stack([dot(pick, grad_out[:, d * half:(d + 1) * half], ((...  5.13 us
    all_to_all x1, starting transfers between devices, on_device(): lax.all_to_all(send_scaled, 'expert', split_axis=0, concat_axis=0, tiled=...  5.01 us
  transfers between devices with their start and end apart: 2, of which 2 were waited for; matrix products, arithmetic and copies ran while one was open for 3% of the time, Pallas kernels for 0%

profile of v1, /device:TPU:1, one launch (start us, length us, event | category | flops | bytes accessed | tf_op | source)
XLA Modules:
  0.0 198.8 jit_solution(17357580117543288955)
XLA Ops:
  3.7 1.5 fusion.4
  5.2 1.5 fusion.3
  6.8 1.7 pad_maximum_fusion
  8.5 5.1 %reshape.52 = bf16[32,20,2048]{2,1,0:T(8,128)(2,1)} reshape(bf16[2,320,2048]{2,1,0:T(8,128)(2,1)} %pad_maximum_fusion) | data formatting | bytes 5242880 | tf_op jit(solution)/shard_map/reshape | solution.py:63
  13.7 78.6 %all_to_all.15 = bf16[32,20,2048]{2,1,0:T(8,128)(2,1)} all-to-all(bf16[32,20,2048]{2,1,0:T(8,128)(2,1)} %reshape.52), channel_id=1, replica_groups=mesh['dp'=2,'expert'=16] {'dp','expert'}, dimensions={0} | all-to-all | bytes 5242880 | tf_op jit(solution)/shard_map/all_to_all | solution.py:67
  92.3 5.2 %reshape.53 = bf16[640,2048]{1,0:T(8,128)(2,1)} reshape(bf16[32,20,2048]{2,1,0:T(8,128)(2,1)} %all_to_all.15) | data formatting | bytes 5242880 | tf_op jit(solution)/shard_map/reshape | solution.py:70
  97.5 4.9 %fusion.5 = bf16[640,768]{1,0:T(8,128)(2,1)} fusion(bf16[640,2048]{1,0:T(8,128)(2,1)} %reshape.53, bf16[1,768,2048]{2,1,0:T(8,128)(2,1)S(1)} %copy-done), kind=kOutput, calls=%fused_computation.9 | convolution fusion | flops 2013757440 | bytes 6750208 | tf_op jit(solution)/shard_map/dot_general | solution.py:40
  102.4 2.1 %reshape.54 = bf16[32,20,768]{2,1,0:T(8,128)(2,1)} reshape(bf16[640,768]{1,0:T(8,128)(2,1)} %fusion.5) | data formatting | bytes 1966080 | tf_op jit(solution)/shard_map/reshape | solution.py:71
  104.5 3.9 %all-to-all-start.1 = ((bf16[32,20,768]{2,1,0:T(8,128)(2,1)}), bf16[32,20,768]{2,1,0:T(8,128)(2,1)}, u32[]{:S(2)}, u32[]{:S(2)}) async-start(bf16[32,20,768]{2,1,0:T(8,128)(2,1)} %reshape.54), calls=%async_computation.1 | async-start | bytes 2359296 | tf_op jit(solution)/shard_map/all_to_all | solution.py:72
  108.5 2.4 %fusion.49 = (bf16[128,2,768]{2,1,0:T(2,128)(2,1)S(1)}, bf16[128,2,768]{2,1,0:T(2,128)(2,1)}) fusion(bf16[128,2,1536]{2,1,0:T(2,128)(2,1)} %param.6), kind=kLoop, calls=%fused_computation.74 | loop fusion | bytes 1572864 | tf_op jit(solution)/shard_map/slice | solution.py:19
  110.9 27.0 %all-to-all-done.1 = bf16[32,20,768]{2,1,0:T(8,128)(2,1)} async-done(((bf16[32,20,768]{2,1,0:T(8,128)(2,1)}), bf16[32,20,768]{2,1,0:T(8,128)(2,1)}, u32[]{:S(2)}, u32[]{:S(2)}) %all-to-all-start.1) | async-done | bytes 983072 | tf_op jit(solution)/shard_map/all_to_all | solution.py:72
  137.9 2.3 %fusion.48 = (bf16[16,20,768]{2,1,0:T(8,128)(2,1)}, bf16[16,20,768]{2,1,0:T(8,128)(2,1)}) fusion(bf16[32,20,768]{2,1,0:T(8,128)(2,1)} %all-to-all-done.1), kind=kLoop, calls=%fused_computation.73 | loop fusion | bytes 1966080 | tf_op jit(solution)/shard_map/slice | solution.py:76
  140.2 1.9 squeeze.18
  142.1 2.1 %fusion.28 = f32[128,768]{1,0:T(8,128)} fusion(bf16[320,768]{1,0:T(8,128)(2,1)} %squeeze.18, s32[128]{0:T(128)S(1)} %get-tuple-element.24), kind=kOutput, calls=%fused_computation.46 | convolution fusion | flops 62955520 | bytes 885248 | tf_op jit(solution)/shard_map/dot_general | solution.py:40
  144.2 2.1 %fusion.30 = f32[128,768]{1,0:T(8,128)} fusion(bf16[320,768]{1,0:T(8,128)(2,1)} %squeeze.18, s32[128]{0:T(128)S(1)} %get-tuple-element.23), kind=kOutput, calls=%fused_computation.49 | convolution fusion | flops 62955520 | bytes 885248 | tf_op jit(solution)/shard_map/dot_general | solution.py:40
  146.3 1.9 squeeze.19
  151.2 3.1 %fusion.15 = (bf16[128,2]{0,1:T(2,128)(2,1)}, bf16[128,2,768]{2,0,1:T(8,128)(2,1)}, bf16[128,2,768]{2,0,1:T(8,128)(2,1)S(1)}, bf16[128,2,768]{2,0,1:T(8,128)(2,1)}) fusion(bf16[128,2,768]{2,1,0:T(2,128)(2,1)S(1)} %get-tuple-element.21, bf16[128,1,768]{2,0,1:T(8,128)(2,1)S(1)} %fusion.11, bf16[128,1,768]{2,0,1:T(8,128)(2,1)S(1)} %fusion.12, ...), kind=kLoop, calls=%fused_computation.28 | loop fusion | flops 5504768 | bytes 2360832 | tf_op jit(solution)/shard_map/reduce_sum | solution.py:26
  155.6 1.9 reshape.55
  157.5 5.0 %all-to-all-start.2 = ((bf16[16,20,768]{2,1,0:T(8,128)(2,1)}), bf16[16,20,768]{2,1,0:T(8,128)(2,1)}, u32[]{:S(2)}, u32[]{:S(2)}) async-start(bf16[16,20,768]{2,1,0:T(8,128)(2,1)} %reshape.55), calls=%async_computation.2 | async-start | bytes 1179648 | tf_op jit(solution)/shard_map/all_to_all | solution.py:68
  163.6 1.7 copy.33
  165.3 12.6 %all-to-all-done.2 = bf16[16,20,768]{2,1,0:T(8,128)(2,1)} async-done(((bf16[16,20,768]{2,1,0:T(8,128)(2,1)}), bf16[16,20,768]{2,1,0:T(8,128)(2,1)}, u32[]{:S(2)}, u32[]{:S(2)}) %all-to-all-start.2) | async-done | bytes 491552 | tf_op jit(solution)/shard_map/all_to_all | solution.py:68
  177.9 1.9 reshape.56
  179.8 13.2 %all_gather.3 = bf16[640,768]{1,0:T(8,128)(2,1)S(1)} all-gather(bf16[320,768]{1,0:T(8,128)(2,1)} %reshape.56), channel_id=1, replica_groups=mesh['dp'=2,'expert'=16] {'dp'}, dimensions={0}, use_global_device_ids=true | all-gather | bytes 1474560 | tf_op jit(solution)/shard_map/all_gather | solution.py:69
  193.0 5.7 %fusion.2 = bf16[1,768,2048]{2,1,0:T(8,128)(2,1)} fusion(bf16[640,768]{1,0:T(8,128)(2,1)S(1)} %all_gather.3, bf16[640,2048]{1,0:T(8,128)(2,1)} %reshape.53), kind=kOutput, calls=%fused_computation.3 | convolution fusion | flops 2014838784 | bytes 6750208 | tf_op jit(solution)/shard_map/dot_general | solution.py:40
  (25 shorter events, 8.4 us)
Async XLA Ops:
  0.6 96.8 %copy-start = (bf16[1,768,2048]{2,1,0:T(8,128)(2,1)S(1)}, bf16[1,768,2048]{2,1,0:T(8,128)(2,1)}, u32[]{:S(2)}) copy-start(bf16[1,768,2048]{2,1,0:T(8,128)(2,1)} %param.9) | copy-start | bytes 9437188
  102.4 6.1 %copy-start.2 = (bf16[128,2]{0,1:T(2,128)(2,1)S(1)}, bf16[128,2]{0,1:T(2,128)(2,1)}, u32[]{:S(2)}) copy-start(bf16[128,2]{0,1:T(2,128)(2,1)} %param.7) | copy-start | bytes 1540
  104.5 33.3 %all-to-all-start.1 = ((bf16[32,20,768]{2,1,0:T(8,128)(2,1)}), bf16[32,20,768]{2,1,0:T(8,128)(2,1)}, u32[]{:S(2)}, u32[]{:S(2)}) async-start(bf16[32,20,768]{2,1,0:T(8,128)(2,1)} %reshape.54), calls=%async_computation.1 | async-start | bytes 2359296 | tf_op jit(solution)/shard_map/all_to_all | solution.py:72
  154.3 8.3 %copy-start.1 = (bf16[128,2,768]{2,0,1:T(8,128)(2,1)S(1)}, bf16[128,2,768]{2,0,1:T(8,128)(2,1)}, u32[]{:S(2)}) copy-start(bf16[128,2,768]{2,0,1:T(8,128)(2,1)} %get-tuple-element.16) | copy-start | bytes 1179652
  157.5 20.4 %all-to-all-start.2 = ((bf16[16,20,768]{2,1,0:T(8,128)(2,1)}), bf16[16,20,768]{2,1,0:T(8,128)(2,1)}, u32[]{:S(2)}, u32[]{:S(2)}) async-start(bf16[16,20,768]{2,1,0:T(8,128)(2,1)} %reshape.55), calls=%async_computation.2 | async-start | bytes 1179648 | tf_op jit(solution)/shard_map/all_to_all | solution.py:68

commit v2 on v1

--- a/solution.py
+++ b/solution.py
@@ -1,6 +1,10 @@
+import functools
+
 import jax
 import jax.numpy as jnp
 from jax import lax
+from jax.experimental import pallas as pl
+from jax.experimental.pallas import tpu as pltpu
 from jax.sharding import PartitionSpec as P
 
 BF16 = jnp.bfloat16
@@ -40,7 +44,7 @@
     return lax.dot_general(a, b, (dims, ((), ())), preferred_element_type=F32)
 
 
-def on_device(grad_out, saved_pre, gate_weight, routes, w_down):
+def on_device_general(grad_out, saved_pre, gate_weight, routes, w_down):
     tokens_dev, top_count = routes.shape
     hidden = w_down.shape[1]
     half = w_down.shape[2]
@@ -83,6 +87,351 @@
     return grads, gate_grad, grad_down[None]
 
 
+BASE = 16
+MESH = pl.DeviceIdType.MESH
+
+
+def iota(shape, axis):
+    return lax.broadcasted_iota(jnp.int32, shape, axis)
+
+
+def unfold_pick(groups, rest, fold, q):
+    shape = (groups * rest, groups * BASE)
+    row, col = iota(shape, 0), iota(shape, 1)
+    return (col == (row // rest) * BASE + q * rest + row % rest).astype(BF16)
+
+
+def fold_pick(groups, rest, fold, q):
+    shape = (groups * BASE, groups * rest)
+    row, col = iota(shape, 0), iota(shape, 1)
+    mine = (row // rest) % fold == q
+    return (mine & (col == (row // BASE) * rest + row % rest)).astype(BF16)
+
+
+def pack_kernel(experts, rest, fold, replicas, s_fold, pos, rows, scaled0, scaled1, main, left, smain, sleft):
+    tokens, width = rows.shape
+    half = width // replicas
+    part = half // fold
+    count = experts * BASE
+    pos0, pos1 = pos[0:1, :], pos[1:2, :]
+    row = iota((count, tokens), 0)
+    pick0, pick1 = (pos0 == row).astype(BF16), (pos1 == row).astype(BF16)
+    both = pick0 + pick1
+    step = 1024
+    for c in range(0, width, step):
+        main[:, c : c + step] = dot(both, rows[:, c : c + step], ((1,), (0,))).astype(BF16)
+    smain[...] = (
+        dot(pick0, scaled0[...], ((1,), (0,))) + dot(pick1, scaled1[...], ((1,), (0,)))
+    ).astype(BF16)
+    slot = count + (row // BASE) * rest + row % rest
+    total = [jnp.zeros((count, part), F32) for _ in range(replicas)]
+    part_s = sleft.shape[1]
+    total_s = jnp.zeros((count, part_s), F32)
+    for q in range(fold):
+        mine = (row // rest) % fold == q
+        q0, q1 = ((pos0 == slot) & mine).astype(BF16), ((pos1 == slot) & mine).astype(BF16)
+        for d in range(replicas):
+            at = d * half + q * part
+            total[d] = total[d] + dot(q0 + q1, rows[:, at : at + part], ((1,), (0,)))
+        if q < s_fold:
+            at = q * part_s
+            total_s = total_s + dot(q0, scaled0[:, at : at + part_s], ((1,), (0,)))
+            total_s = total_s + dot(q1, scaled1[:, at : at + part_s], ((1,), (0,)))
+    for d in range(replicas):
+        left[:, d * part : (d + 1) * part] = total[d].astype(BF16)
+    sleft[...] = total_s.astype(BF16)
+
+
+def exchange_kernel(
+    experts, rest, fold, s_fold,
+    main, left, smain, sleft, w_hbm,
+    ret_out, grad_out,
+    w, x_main, x_left, z, s_main, s_left, s_rest, s_turn, s_turn_rest,
+    mine_f32, out_px, in_px, out_pl, in_pl, c_main, c_left, r_main, r_left,
+    w_sem, tx, rx, txl, rxl, ts, rs, tsl, rsl, tp, rp, tc, rc, tcl, rcl,
+):
+    d = lax.axis_index("dp")
+    e = lax.axis_index("expert")
+    other = 1 - d
+    devices = 2 * experts
+    me = d * experts + e
+    half = w.shape[1]
+    part = half // fold
+    hidden = w.shape[0]
+    part_s = sleft.shape[1]
+    own, rest_own = experts * BASE, experts * rest
+
+    def block(i):
+        return pl.ds(pl.multiple_of(i * BASE, BASE), BASE)
+
+    def remote(src, dst, send, recv, to):
+        return pltpu.make_async_remote_copy(
+            src_ref=src, dst_ref=dst, send_sem=send, recv_sem=recv, device_id=to, device_id_type=MESH
+        )
+
+    def row_copies(p, s):
+        pd, pe = p // experts, p % experts
+        wide = pl.ds(pl.multiple_of(pd * half, 128), half)
+        narrow = pl.ds(pl.multiple_of(pd * part, 128), part)
+        return (
+            remote(main.at[block(pe), wide], x_main.at[block(s)], tx.at[p], rx.at[s], (pd, pe)),
+            remote(left.at[block(pe), narrow], x_left.at[block(s)], txl.at[p], rxl.at[s], (pd, pe)),
+        )
+
+    def scaled_copies(pe, se):
+        s = d * experts + se
+        return (
+            remote(smain.at[block(pe)], s_main.at[block(s)], ts.at[pe], rs.at[se], (d, pe)),
+            remote(sleft.at[block(pe)], s_left.at[block(s)], tsl.at[pe], rsl.at[se], (d, pe)),
+        )
+
+    def back_copies(pe, se):
+        return (
+            remote(c_main.at[block(pe)], r_main.at[block(se)], tc.at[pe], rc.at[se], (d, pe)),
+            remote(c_left.at[block(pe)], r_left.at[block(se)], tcl.at[pe], rcl.at[se], (d, pe)),
+        )
+
+    def each(count, position, body):
+        def step(k, carry):
+            body((position + k) % count)
+            return carry
+
+        lax.fori_loop(1, count, step, 0)
+
+    fetch_w = pltpu.make_async_copy(w_hbm, w, w_sem)
+    fetch_w.start()
+    barrier = pltpu.get_barrier_semaphore()
+
+    def greet(p):
+        pl.semaphore_signal(
+            barrier, inc=1, device_id=(p // experts, p % experts), device_id_type=MESH
+        )
+
+    each(devices, me, greet)
+    pl.semaphore_wait(barrier, devices - 1)
+
+    def start_rows(p):
+        for copy in row_copies(p, me):
+            copy.start()
+
+    each(devices, me, start_rows)
+
+    def start_scaled(p):
+        for copy in scaled_copies(p, e):
+            copy.start()
+
+    each(experts, e, start_scaled)
+    kept = [
+        pltpu.make_async_copy(
+            main.at[block(e), pl.ds(pl.multiple_of(d * half, 128), half)], x_main.at[block(me)], rx.at[me]
+        ),
+        pltpu.make_async_copy(
+            left.at[block(e), pl.ds(pl.multiple_of(d * part, 128), part)], x_left.at[block(me)], rxl.at[me]
+        ),
+        pltpu.make_async_copy(smain.at[block(e)], s_main.at[block(me)], rs.at[e]),
+        pltpu.make_async_copy(sleft.at[block(e)], s_left.at[block(me)], rsl.at[e]),
+    ]
+    for copy in kept:
+        copy.start()
+    for copy in kept:
+        copy.wait()
+    fetch_w.wait()
+
+    def wait_rows(s):
+        for copy in row_copies(s, s):
+            copy.wait_recv()
+
+    each(devices, me, wait_rows)
+
+    for q in range(fold):
+        z[:, q * part : (q + 1) * part] = dot(
+            unfold_pick(devices, rest, fold, q), x_left[...], ((1,), (0,))
+        ).astype(BF16)
+
+    def contract(lo, ref, rows, start):
+        return dot(ref[pl.ds(start, rows), :], w[lo : lo + 256, :], ((1,), (1,)))
+
+    other_at, own_at = pl.multiple_of(other * own, own), pl.multiple_of(d * own, own)
+    other_rest, own_rest = pl.multiple_of(other * rest_own, rest_own), pl.multiple_of(d * rest_own, rest_own)
+    for lo in range(0, hidden, 256):
+        out_px[:, lo : lo + 256] = contract(lo, x_main, own, other_at).astype(BF16)
+        out_pl[:, lo : lo + 256] = contract(lo, z, rest_own, other_rest).astype(BF16)
+    across = (other, e)
+    px = remote(out_px, in_px, tp.at[0], rp.at[0], across)
+    plx = remote(out_pl, in_pl, tp.at[1], rp.at[1], across)
+    px.start()
+    plx.start()
+    for lo in range(0, hidden, 256):
+        mine_f32[0:own, lo : lo + 256] = contract(lo, x_main, own, own_at)
+        mine_f32[own : own + rest_own, lo : lo + 256] = contract(lo, z, rest_own, own_rest)
+    px.wait()
+    plx.wait()
+    c_main[...] = (mine_f32[0:own, :] + in_px[...].astype(F32)).astype(BF16)
+    c_rest = (mine_f32[own : own + rest_own, :] + in_pl[...].astype(F32)).astype(BF16)
+    folded = jnp.zeros((own, part_s), F32)
+    for q in range(s_fold):
+        folded = folded + dot(
+            fold_pick(experts, rest, fold, q), c_rest[:, q * part_s : (q + 1) * part_s], ((1,), (0,))
+        )
+    c_left[...] = folded.astype(BF16)
+
+    def start_back(p):
+        for copy in back_copies(p, e):
+            copy.start()
+
+    each(experts, e, start_back)
+    kept_back = [
+        pltpu.make_async_copy(c_main.at[block(e)], r_main.at[block(e)], rc.at[e]),
+        pltpu.make_async_copy(c_left.at[block(e)], r_left.at[block(e)], rcl.at[e]),
+    ]
+    for copy in kept_back:
+        copy.start()
+
+    def wait_scaled(s):
+        for copy in scaled_copies(s, s):
+            copy.wait_recv()
+
+    each(experts, e, wait_scaled)
+    region = pl.ds(own_at, own)
+    forward = [
+        remote(s_main.at[region], s_main.at[region], tp.at[2], rp.at[2], across),
+        remote(s_left.at[region], s_left.at[region], tp.at[3], rp.at[3], across),
+    ]
+    for copy in forward:
+        copy.start()
+    for copy in forward:
+        copy.wait()
+    for q in range(s_fold):
+        s_rest[:, q * part_s : (q + 1) * part_s] = dot(
+            unfold_pick(devices, rest, fold, q), s_left[...], ((1,), (0,))
+        ).astype(BF16)
+    s_turn[...] = s_main[...].T
+    s_turn_rest[...] = s_rest[...].T
+
+    @pl.loop(0, half // 512)
+    def _(j):
+        columns = pl.ds(pl.multiple_of(j * 512, 512), 512)
+        grad_out[:, columns] = (
+            dot(s_turn[...], x_main[:, columns], ((1,), (0,)))
+            + dot(s_turn_rest[...], z[:, columns], ((1,), (0,)))
+        ).astype(BF16)
+
+    for copy in kept_back:
+        copy.wait()
+
+    def wait_back(s):
+        for copy in back_copies(s, s):
+            copy.wait_recv()
+
+    each(experts, e, wait_back)
+    ret_out[0:own, :] = r_main[...]
+    for q in range(s_fold):
+        ret_out[own : own + rest_own, q * part_s : (q + 1) * part_s] = dot(
+            unfold_pick(experts, rest, fold, q), r_left[...], ((1,), (0,))
+        ).astype(BF16)
+
+    def drain_rows(p):
+        for copy in row_copies(p, me):
+            copy.wait_send()
+
+    each(devices, me, drain_rows)
+
+    def drain(p):
+        for copy in scaled_copies(p, e) + back_copies(p, e):
+            copy.wait_send()
+
+    each(experts, e, drain)
+
+
+def on_device(grad_out, saved_pre, gate_weight, routes, w_down):
+    tokens, top_count = routes.shape
+    hidden, half = w_down.shape[1:]
+    width = grad_out.shape[1]
+    experts = lax.axis_size("expert")
+    replicas = lax.axis_size("dp")
+    capacity = 5 * tokens * top_count // (4 * experts)
+    if (replicas, top_count, capacity, hidden % 256, half % 512) != (2, 2, 20, 0, 0):
+        return on_device_general(grad_out, saved_pre, gate_weight, routes, w_down)
+    rest = capacity - BASE
+    fold = BASE // rest
+    s_fold = hidden // 256
+    own, rest_own = experts * BASE, experts * rest
+    devices = replicas * experts
+    expert_ids = jnp.arange(experts, dtype=jnp.int32)
+    named = [(routes[:, k][:, None] == expert_ids[None, :]).astype(F32) for k in range(2)]
+    before = (jnp.arange(tokens)[:, None] > jnp.arange(tokens)[None, :]).astype(BF16)
+    counts = dot(before, (named[0] + named[1]).astype(BF16), ((1,), (0,)))
+    positions = []
+    for k in range(2):
+        rank = jnp.sum(counts * named[k], axis=1).astype(jnp.int32)
+        expert = routes[:, k]
+        positions.append(
+            jnp.where(rank < BASE, expert * BASE + rank, own + expert * rest + rank - BASE)
+        )
+    scaled = [
+        scaled_hidden(saved_pre[:, k], gate_weight[:, k], hidden) for k in range(2)
+    ]
+    vmem = pl.BlockSpec(memory_space=pltpu.VMEM)
+    packed = pl.pallas_call(
+        functools.partial(pack_kernel, experts, rest, fold, replicas, s_fold),
+        out_shape=(
+            jax.ShapeDtypeStruct((own, width), BF16),
+            jax.ShapeDtypeStruct((own, width // fold), BF16),
+            jax.ShapeDtypeStruct((own, hidden), BF16),
+            jax.ShapeDtypeStruct((own, 256), BF16),
+        ),
+        in_specs=[vmem] * 4,
+        out_specs=[vmem] * 4,
+    )(jnp.stack(positions), grad_out, scaled[0], scaled[1])
+    dma = pltpu.SemaphoreType.DMA
+    total = devices * BASE
+    back, grad_down = pl.pallas_call(
+        functools.partial(exchange_kernel, experts, rest, fold, s_fold),
+        out_shape=(
+            jax.ShapeDtypeStruct((own + rest_own, hidden), BF16),
+            jax.ShapeDtypeStruct((hidden, half), BF16),
+        ),
+        in_specs=[vmem] * 4 + [pl.BlockSpec(memory_space=pl.ANY)],
+        out_specs=[vmem] * 2,
+        scratch_shapes=[
+            pltpu.VMEM((hidden, half), BF16),
+            pltpu.VMEM((total, half), BF16),
+            pltpu.VMEM((total, half // fold), BF16),
+            pltpu.VMEM((devices * rest, half), BF16),
+            pltpu.VMEM((total, hidden), BF16),
+            pltpu.VMEM((total, 256), BF16),
+            pltpu.VMEM((devices * rest, hidden), BF16),
+            pltpu.VMEM((hidden, total), BF16),
+            pltpu.VMEM((hidden, devices * rest), BF16),
+            pltpu.VMEM((own + rest_own, hidden), F32),
+            pltpu.VMEM((own, hidden), BF16),
+            pltpu.VMEM((own, hidden), BF16),
+            pltpu.VMEM((rest_own, hidden), BF16),
+            pltpu.VMEM((rest_own, hidden), BF16),
+            pltpu.VMEM((own, hidden), BF16),
+            pltpu.VMEM((own, 256), BF16),
+            pltpu.VMEM((own, hidden), BF16),
+            pltpu.VMEM((own, 256), BF16),
+            dma,
+            dma((devices,)), dma((devices,)), dma((devices,)), dma((devices,)),
+            dma((experts,)), dma((experts,)), dma((experts,)), dma((experts,)),
+            dma((4,)), dma((4,)),
+            dma((experts,)), dma((experts,)), dma((experts,)), dma((experts,)),
+        ],
+        compiler_params=pltpu.CompilerParams(collective_id=0, has_side_effects=True),
+    )(*packed, w_down[0])
+    slot_ids = jnp.arange(own + rest_own, dtype=jnp.int32)
+    contraction = jnp.stack(
+        [
+            dot((positions[k][:, None] == slot_ids[None, :]).astype(BF16), back, ((1,), (0,))).astype(BF16)
+            for k in range(2)
+        ],
+        axis=1,
+    )
+    grads, gate_grad = swiglu_grads(saved_pre, gate_weight, contraction, hidden)
+    return grads, gate_grad, grad_down[None]
+
+
 def solution(mesh):
     return jax.shard_map(
         on_device,

time: 201 us -> 132 us (0.66)
  the two profiles are of different devices: /device:TPU:1 before, /device:TPU:11 now
where the time goes in v2:
time: 132 us
  Pallas kernels  116 us (88%)
  local copies, waits for them, and re-layouts  7.51 us (6%)
  other arithmetic  4.29 us (3%)
  matrix products  2.83 us (2%)
    pallas_call x1, Pallas kernels, on_device(): pl.pallas_call(functools.partial(exchange_kernel, experts, rest, fold, s_...  113 us
    pallas_call x1, Pallas kernels, on_device(): pl.pallas_call(functools.partial(pack_kernel, experts, rest, fold, replic...  3.93 us
    unnamed x10, local copies, waits for them, and re-layouts  3.37 us
    dot_general x3, matrix products, dot(): return lax.dot_general(a, b, (dims, ((), ())), preferred_element_type=F32)  2.83 us
    slice x1, local copies, waits for them, and re-layouts, on_device(): saved_pre[:, k]  2.73 us

profile of v2, /device:TPU:11, one launch (start us, length us, event | category | flops | bytes accessed | tf_op | source)
XLA Modules:
  0.0 131.8 jit_solution(14474974388343486284)
XLA Ops:
  0.6 0.8 slice_bitcast_fusion.1
  1.4 0.2 select_reduce_fusion.1
  1.5 0.8 compare_select_fusion.2
  2.3 0.6 pad_add_fusion.pos
  2.9 0.0 copy-start.3
  2.9 2.7 %fusion.37 = (bf16[128,1,1536]{2,1,0:T(2,128)(2,1)S(1)}, bf16[128,1,1536]{2,1,0:T(2,128)(2,1)S(1)}) fusion(bf16[128,2,1536]{2,1,0:T(2,128)(2,1)} %param.6), kind=kLoop, calls=%fused_computation.81 | loop fusion | bytes 1572864 | tf_op jit(solution)/shard_map/slice | solution.py:372
  5.6 0.1 copy_bitcast_fusion
  5.7 0.0 copy-done.3
  5.8 0.9 fusion.23.scaled1
  6.6 0.8 fusion.24.scaled0
  7.4 3.9 %shard_map.76 = (bf16[256,4096]{1,0:T(8,128)(2,1)}, bf16[256,1024]{1,0:T(8,128)(2,1)}, bf16[256,768]{1,0:T(8,128)(2,1)}, bf16[256,256]{1,0:T(8,128)(2,1)}) custom-call(s32[2,128]{1,0:T(2,128)} %pad_add_fusion.pos, bf16[128,4096]{1,0:T(8,128)(2,1)} %rows.1, bf16[128,768]{1,0:T(8,128)(2,1)} %fusion.24.scaled0, bf16[128,768]{1,0:T(8,128)(2,1)} %fusion.23.scaled1), custom_call_target="tpu_custom_call" | custom-call | tf_op jit(solution)/shard_map/pallas_call | solution.py:375
  11.4 0.0 copy-start.2
  11.4 112.5 %shard_map.77 = (bf16[320,768]{1,0:T(8,128)(2,1)}, bf16[768,2048]{1,0:T(8,128)(2,1)}) custom-call(bf16[256,4096]{1,0:T(8,128)(2,1)} %get-tuple-element.9.main, bf16[256,1024]{1,0:T(8,128)(2,1)} %get-tuple-element.10.left, bf16[256,768]{1,0:T(8,128)(2,1)} %get-tuple-element.11.smain, bf16[256,256]{1,0:T(8,128)(2,1)} %get-tuple-element.12.sleft, ...), custom_call_target="tpu_custom_call" | custom-call | tf_op jit(solution)/shard_map/pallas_call | solution.py:388
  123.9 0.0 copy-done.2
  123.9 1.3 %fusion = bf16[128,1,768]{2,0,1:T(8,128)(2,1)S(1)} fusion(bf16[320,768]{1,0:T(8,128)(2,1)} %get-tuple-element.13, s32[128]{0:T(128)S(1)} %get-tuple-element.27), kind=kOutput, calls=%fused_computation.5 | convolution fusion | flops 63053824 | bytes 688640 | tf_op jit(solution)/shard_map/dot_general | solution.py:44
  125.3 1.3 %fusion.1 = bf16[128,1,768]{2,0,1:T(8,128)(2,1)S(1)} fusion(bf16[320,768]{1,0:T(8,128)(2,1)} %get-tuple-element.13, s32[128]{0:T(128)S(1)} %get-tuple-element.28), kind=kOutput, calls=%fused_computation.6 | convolution fusion | flops 63053824 | bytes 688640 | tf_op jit(solution)/shard_map/dot_general | solution.py:44
  126.6 0.0 copy-done
  126.6 0.5 fusion.36
  127.2 0.0 copy-start.1
  127.2 1.2 fusion.4
  128.4 0.1 pad_maximum_fusion
  128.5 1.7 %copy.12 = bf16[128,2,1536]{2,1,0:T(2,128)(2,1)} copy(bf16[128,2,1536]{2,0,1:T(8,128)(2,1)S(1)} %pad_maximum_fusion) | data formatting | bytes 1572864
  130.1 0.0 copy-done.1
  130.1 1.7 %copy.28 = bf16[1,768,2048]{2,1,0:T(8,128)(2,1)} copy(bf16[1,768,2048]{2,1,0:T(8,128)(2,1)S(1)} %bitcast.71) | data formatting | bytes 6291456
  (4 shorter events, 0.0 us)
Async XLA Ops:
  2.9 2.9 %copy-start.3 = (bf16[128,2]{0,1:T(2,128)(2,1)S(1)}, bf16[128,2]{0,1:T(2,128)(2,1)}, u32[]{:S(2)}) copy-start(bf16[128,2]{0,1:T(2,128)(2,1)} %param.7) | copy-start | bytes 1540
  11.4 112.5 %copy-start.2 = (s32[128,2]{0,1:T(2,128)S(1)}, s32[128,2]{0,1:T(2,128)}, u32[]{:S(2)}) copy-start(s32[128,2]{0,1:T(2,128)} %param.8) | copy-start | bytes 3076
  11.4 115.2 %copy-start = (bf16[128,2,1536]{2,1,0:T(2,128)(2,1)S(1)}, bf16[128,2,1536]{2,1,0:T(2,128)(2,1)}, u32[]{:S(2)}) copy-start(bf16[128,2,1536]{2,1,0:T(2,128)(2,1)} %param.6) | copy-start | bytes 2359300
  127.2 3.0 %copy-start.1 = (bf16[768,2048]{1,0:T(8,128)(2,1)S(1)}, bf16[768,2048]{1,0:T(8,128)(2,1)}, u32[]{:S(2)}) copy-start(bf16[768,2048]{1,0:T(8,128)(2,1)} %get-tuple-element.14) | copy-start | bytes 9437188

commit v3 on v2

--- a/solution.py
+++ b/solution.py
@@ -108,11 +108,25 @@
     return (mine & (col == (row // BASE) * rest + row % rest)).astype(BF16)
 
 
-def pack_kernel(experts, rest, fold, replicas, s_fold, pos, rows, scaled0, scaled1, main, left, smain, sleft):
+def pack_kernel(
+    experts, rest, fold, replicas, s_fold,
+    routes, rows, scaled0, scaled1,
+    main, left, smain, sleft, pos,
+):
     tokens, width = rows.shape
     half = width // replicas
     part = half // fold
     count = experts * BASE
+    names = iota((experts, tokens), 0)
+    named = [(routes[k : k + 1, :] == names).astype(F32) for k in range(2)]
+    before = (iota((tokens, tokens), 0) < iota((tokens, tokens), 1)).astype(BF16)
+    counts = dot((named[0] + named[1]).astype(BF16), before, ((1,), (0,)))
+    for k in range(2):
+        rank = jnp.sum(counts * named[k], axis=0, keepdims=True).astype(jnp.int32)
+        expert = routes[k : k + 1, :]
+        pos[k : k + 1, :] = jnp.where(
+            rank < BASE, expert * BASE + rank, count + expert * rest + rank - BASE
+        )
     pos0, pos1 = pos[0:1, :], pos[1:2, :]
     row = iota((count, tokens), 0)
     pick0, pick1 = (pos0 == row).astype(BF16), (pos1 == row).astype(BF16)
@@ -193,7 +207,7 @@
 
     def each(count, position, body):
         def step(k, carry):
-            body((position + k) % count)
+            body((position + 1 + (k + count // 2 - 1) % (count - 1)) % count)
             return carry
 
         lax.fori_loop(1, count, step, 0)
@@ -210,17 +224,24 @@
     each(devices, me, greet)
     pl.semaphore_wait(barrier, devices - 1)
 
-    def start_rows(p):
-        for copy in row_copies(p, me):
+    def start_across(k, carry):
+        for copy in row_copies(other * experts + (e + experts // 2 + k) % experts, me):
             copy.start()
-
-    each(devices, me, start_rows)
+        return carry
+
+    lax.fori_loop(0, experts, start_across, 0)
 
     def start_scaled(p):
         for copy in scaled_copies(p, e):
             copy.start()
 
     each(experts, e, start_scaled)
+
+    def start_rows(p):
+        for copy in row_copies(d * experts + p, me):
+            copy.start()
+
+    each(experts, e, start_rows)
     kept = [
         pltpu.make_async_copy(
             main.at[block(e), pl.ds(pl.multiple_of(d * half, 128), half)], x_main.at[block(me)], rx.at[me]
@@ -237,22 +258,26 @@
         copy.wait()
     fetch_w.wait()
 
-    def wait_rows(s):
+    other_at, own_at = pl.multiple_of(other * own, own), pl.multiple_of(d * own, own)
+    other_rest, own_rest = pl.multiple_of(other * rest_own, rest_own), pl.multiple_of(d * rest_own, rest_own)
+
+    def unfold_rows(at, rest_at):
+        for q in range(fold):
+            z[pl.ds(rest_at, rest_own), q * part : (q + 1) * part] = dot(
+                unfold_pick(experts, rest, fold, q), x_left[pl.ds(at, own), :], ((1,), (0,))
+            ).astype(BF16)
+
+    def contract(lo, ref, rows, start):
+        return dot(ref[pl.ds(start, rows), :], w[lo : lo + 256, :], ((1,), (1,)))
+
+    def wait_across(k, carry):
+        s = other * experts + k
         for copy in row_copies(s, s):
             copy.wait_recv()
-
-    each(devices, me, wait_rows)
-
-    for q in range(fold):
-        z[:, q * part : (q + 1) * part] = dot(
-            unfold_pick(devices, rest, fold, q), x_left[...], ((1,), (0,))
-        ).astype(BF16)
-
-    def contract(lo, ref, rows, start):
-        return dot(ref[pl.ds(start, rows), :], w[lo : lo + 256, :], ((1,), (1,)))
-
-    other_at, own_at = pl.multiple_of(other * own, own), pl.multiple_of(d * own, own)
-    other_rest, own_rest = pl.multiple_of(other * rest_own, rest_own), pl.multiple_of(d * rest_own, rest_own)
+        return carry
+
+    lax.fori_loop(0, experts, wait_across, 0)
+    unfold_rows(other_at, other_rest)
     for lo in range(0, hidden, 256):
         out_px[:, lo : lo + 256] = contract(lo, x_main, own, other_at).astype(BF16)
         out_pl[:, lo : lo + 256] = contract(lo, z, rest_own, other_rest).astype(BF16)
@@ -261,31 +286,6 @@
     plx = remote(out_pl, in_pl, tp.at[1], rp.at[1], across)
     px.start()
     plx.start()
-    for lo in range(0, hidden, 256):
-        mine_f32[0:own, lo : lo + 256] = contract(lo, x_main, own, own_at)
-        mine_f32[own : own + rest_own, lo : lo + 256] = contract(lo, z, rest_own, own_rest)
-    px.wait()
-    plx.wait()
-    c_main[...] = (mine_f32[0:own, :] + in_px[...].astype(F32)).astype(BF16)
-    c_rest = (mine_f32[own : own + rest_own, :] + in_pl[...].astype(F32)).astype(BF16)
-    folded = jnp.zeros((own, part_s), F32)
-    for q in range(s_fold):
-        folded = folded + dot(
-            fold_pick(experts, rest, fold, q), c_rest[:, q * part_s : (q + 1) * part_s], ((1,), (0,))
-        )
-    c_left[...] = folded.astype(BF16)
-
-    def start_back(p):
-        for copy in back_copies(p, e):
-            copy.start()
-
-    each(experts, e, start_back)
-    kept_back = [
-        pltpu.make_async_copy(c_main.at[block(e)], r_main.at[block(e)], rc.at[e]),
-        pltpu.make_async_copy(c_left.at[block(e)], r_left.at[block(e)], rcl.at[e]),
-    ]
-    for copy in kept_back:
-        copy.start()
 
     def wait_scaled(s):
         for copy in scaled_copies(s, s):
@@ -299,6 +299,8 @@
     ]
     for copy in forward:
         copy.start()
+    px.wait()
+    plx.wait()
     for copy in forward:
         copy.wait()
     for q in range(s_fold):
@@ -307,6 +309,37 @@
         ).astype(BF16)
     s_turn[...] = s_main[...].T
     s_turn_rest[...] = s_rest[...].T
+
+    def wait_rows(p):
+        s = d * experts + p
+        for copy in row_copies(s, s):
+            copy.wait_recv()
+
+    each(experts, e, wait_rows)
+    unfold_rows(own_at, own_rest)
+    for lo in range(0, hidden, 256):
+        cut = slice(lo, lo + 256)
+        c_main[:, cut] = (contract(lo, x_main, own, own_at) + in_px[:, cut].astype(F32)).astype(BF16)
+        mine_f32[:, cut] = contract(lo, z, rest_own, own_rest)
+    c_rest = (mine_f32[...] + in_pl[...].astype(F32)).astype(BF16)
+    folded = jnp.zeros((own, part_s), F32)
+    for q in range(s_fold):
+        folded = folded + dot(
+            fold_pick(experts, rest, fold, q), c_rest[:, q * part_s : (q + 1) * part_s], ((1,), (0,))
+        )
+    c_left[...] = folded.astype(BF16)
+
+    def start_back(p):
+        for copy in back_copies(p, e):
+            copy.start()
+
+    each(experts, e, start_back)
+    kept_back = [
+        pltpu.make_async_copy(c_main.at[block(e)], r_main.at[block(e)], rc.at[e]),
+        pltpu.make_async_copy(c_left.at[block(e)], r_left.at[block(e)], rcl.at[e]),
+    ]
+    for copy in kept_back:
+        copy.start()
 
     @pl.loop(0, half // 512)
     def _(j):
@@ -357,32 +390,22 @@
     s_fold = hidden // 256
     own, rest_own = experts * BASE, experts * rest
     devices = replicas * experts
-    expert_ids = jnp.arange(experts, dtype=jnp.int32)
-    named = [(routes[:, k][:, None] == expert_ids[None, :]).astype(F32) for k in range(2)]
-    before = (jnp.arange(tokens)[:, None] > jnp.arange(tokens)[None, :]).astype(BF16)
-    counts = dot(before, (named[0] + named[1]).astype(BF16), ((1,), (0,)))
-    positions = []
-    for k in range(2):
-        rank = jnp.sum(counts * named[k], axis=1).astype(jnp.int32)
-        expert = routes[:, k]
-        positions.append(
-            jnp.where(rank < BASE, expert * BASE + rank, own + expert * rest + rank - BASE)
-        )
     scaled = [
         scaled_hidden(saved_pre[:, k], gate_weight[:, k], hidden) for k in range(2)
     ]
     vmem = pl.BlockSpec(memory_space=pltpu.VMEM)
-    packed = pl.pallas_call(
+    *packed, positions = pl.pallas_call(
         functools.partial(pack_kernel, experts, rest, fold, replicas, s_fold),
         out_shape=(
             jax.ShapeDtypeStruct((own, width), BF16),
             jax.ShapeDtypeStruct((own, width // fold), BF16),
             jax.ShapeDtypeStruct((own, hidden), BF16),
             jax.ShapeDtypeStruct((own, 256), BF16),
+            jax.ShapeDtypeStruct((2, tokens), jnp.int32),
         ),
         in_specs=[vmem] * 4,
-        out_specs=[vmem] * 4,
-    )(jnp.stack(positions), grad_out, scaled[0], scaled[1])
+        out_specs=[vmem] * 5,
+    )(routes.T, grad_out, scaled[0], scaled[1])
     dma = pltpu.SemaphoreType.DMA
     total = devices * BASE
     back, grad_down = pl.pallas_call(
@@ -403,7 +426,7 @@
             pltpu.VMEM((devices * rest, hidden), BF16),
             pltpu.VMEM((hidden, total), BF16),
             pltpu.VMEM((hidden, devices * rest), BF16),
-            pltpu.VMEM((own + rest_own, hidden), F32),
+            pltpu.VMEM((rest_own, hidden), F32),
             pltpu.VMEM((own, hidden), BF16),
             pltpu.VMEM((own, hidden), BF16),
             pltpu.VMEM((rest_own, hidden), BF16),
@@ -421,13 +444,9 @@
         compiler_params=pltpu.CompilerParams(collective_id=0, has_side_effects=True),
     )(*packed, w_down[0])
     slot_ids = jnp.arange(own + rest_own, dtype=jnp.int32)
-    contraction = jnp.stack(
-        [
-            dot((positions[k][:, None] == slot_ids[None, :]).astype(BF16), back, ((1,), (0,))).astype(BF16)
-            for k in range(2)
-        ],
-        axis=1,
-    )
+    pick = (positions[:, :, None] == slot_ids).astype(BF16).reshape(2 * tokens, -1)
+    contraction = dot(pick, back, ((1,), (0,))).astype(BF16).reshape(2, tokens, hidden)
+    contraction = jnp.stack([contraction[0], contraction[1]], axis=1)
     grads, gate_grad = swiglu_grads(saved_pre, gate_weight, contraction, hidden)
     return grads, gate_grad, grad_down[None]
 

time: 132 us -> 118 us (0.89)
  the two profiles are of different devices: /device:TPU:11 before, /device:TPU:1 now
where the time goes in v3:
time: 118 us
  Pallas kernels  106 us (90%)
  local copies, waits for them, and re-layouts  6.77 us (6%)
  other arithmetic  2.93 us (2%)
  matrix products  1.51 us (1%)
    pallas_call x1, Pallas kernels, on_device(): pl.pallas_call(functools.partial(exchange_kernel, experts, rest, fold, s_...  102 us
    pallas_call x1, Pallas kernels, on_device(): pl.pallas_call(functools.partial(pack_kernel, experts, rest, fold, replic...  4.13 us
    unnamed x10, local copies, waits for them, and re-layouts  3.37 us
    slice x1, local copies, waits for them, and re-layouts, on_device(): saved_pre[:, k]  2.73 us

profile of v3, /device:TPU:1, one launch (start us, length us, event | category | flops | bytes accessed | tf_op | source)
XLA Modules:
  0.0 117.7 jit_solution(12461450820734059247)
XLA Ops:
  0.6 0.0 copy-start.2
  0.6 2.7 %fusion.25 = (bf16[128,1,1536]{2,1,0:T(2,128)(2,1)S(1)}, bf16[128,1,1536]{2,1,0:T(2,128)(2,1)S(1)}) fusion(bf16[128,2,1536]{2,1,0:T(2,128)(2,1)} %param.6), kind=kLoop, calls=%fused_computation.46 | loop fusion | bytes 1572864 | tf_op jit(solution)/shard_map/slice | solution.py:394
  3.4 0.1 copy_bitcast_fusion
  3.5 0.0 copy-done.2
  3.5 0.8 fusion.21.scaled1
  4.3 0.8 fusion.22.scaled0
  5.2 4.1 %shard_map.76 = (bf16[256,4096]{1,0:T(8,128)(2,1)}, bf16[256,1024]{1,0:T(8,128)(2,1)}, bf16[256,768]{1,0:T(8,128)(2,1)}, bf16[256,256]{1,0:T(8,128)(2,1)}, s32[2,128]{1,0:T(2,128)}) custom-call(s32[2,128]{1,0:T(2,128)} %bitcast.21, bf16[128,4096]{1,0:T(8,128)(2,1)} %rows.1, bf16[128,768]{1,0:T(8,128)(2,1)} %fusion.22.scaled0, bf16[128,768]{1,0:T(8,128)(2,1)} %fusion.21.scaled1), custom_call_target="tpu_custom_call" | custom-call | tf_op jit(solution)/shard_map/pallas_call | solution.py:397
  9.3 0.0 copy-start.3
  9.3 101.6 %shard_map.77 = (bf16[320,768]{1,0:T(8,128)(2,1)}, bf16[768,2048]{1,0:T(8,128)(2,1)}) custom-call(bf16[256,4096]{1,0:T(8,128)(2,1)} %get-tuple-element.11.main, bf16[256,1024]{1,0:T(8,128)(2,1)} %get-tuple-element.12.left, bf16[256,768]{1,0:T(8,128)(2,1)} %get-tuple-element.13.smain, bf16[256,256]{1,0:T(8,128)(2,1)} %get-tuple-element.14.sleft, ...), custom_call_target="tpu_custom_call" | custom-call | tf_op jit(solution)/shard_map/pallas_call | solution.py:411
  110.9 0.0 copy-start
  110.9 0.0 copy-done.3
  110.9 1.5 %convolution_convert_fusion = bf16[256,768]{1,0:T(8,128)(2,1)S(1)} fusion(bf16[320,768]{1,0:T(8,128)(2,1)} %get-tuple-element.15, s32[256]{0:T(256)S(1)} %bitcast.22), kind=kOutput, calls=%fused_computation | convolution fusion | flops 126107648 | bytes 885760 | tf_op jit(solution)/shard_map/dot_general | solution.py:44
  112.5 0.0 copy-done
  112.5 0.5 fusion.24
  113.1 0.0 copy-start.1
  113.1 1.2 %fusion.2 = (bf16[128,2]{0,1:T(2,128)(2,1)}, bf16[128,2,768]{2,0,1:T(8,128)(2,1)S(1)}, bf16[128,2,768]{2,0,1:T(8,128)(2,1)S(1)}) fusion(bf16[128,2,768]{2,1,0:T(2,128)(2,1)S(1)} %get-tuple-element.23, bf16[128,2,768]{2,1,0:T(2,128)(2,1)S(1)} %get-tuple-element.24, bf16[128,1,768]{2,0,1:T(8,128)(2,1)S(1)} %get-tuple-element.28, ...), kind=kLoop, calls=%fused_computation.10 | loop fusion | flops 4914944 | bytes 1967616 | tf_op jit(solution)/shard_map/reduce_sum | solution.py:30
  114.3 0.1 pad_maximum_fusion
  114.3 1.7 %copy.12 = bf16[128,2,1536]{2,1,0:T(2,128)(2,1)} copy(bf16[128,2,1536]{2,0,1:T(8,128)(2,1)S(1)} %pad_maximum_fusion) | data formatting | bytes 1572864
  116.0 0.0 copy-done.1
  116.0 1.7 %copy.28 = bf16[1,768,2048]{2,1,0:T(8,128)(2,1)} copy(bf16[1,768,2048]{2,1,0:T(8,128)(2,1)S(1)} %bitcast.20) | data formatting | bytes 6291456
  (3 shorter events, 0.0 us)
Async XLA Ops:
  0.6 2.9 %copy-start.2 = (bf16[128,2]{0,1:T(2,128)(2,1)S(1)}, bf16[128,2]{0,1:T(2,128)(2,1)}, u32[]{:S(2)}) copy-start(bf16[128,2]{0,1:T(2,128)(2,1)} %param.7) | copy-start | bytes 1540
  9.3 101.6 %copy-start.3 = (s32[2,128]{1,0:T(2,128)S(1)}, s32[2,128]{1,0:T(2,128)}, u32[]{:S(2)}) copy-start(s32[2,128]{1,0:T(2,128)} %get-tuple-element.10) | copy-start | bytes 3076
  110.9 1.6 %copy-start = (bf16[128,2,1536]{2,1,0:T(2,128)(2,1)S(1)}, bf16[128,2,1536]{2,1,0:T(2,128)(2,1)}, u32[]{:S(2)}) copy-start(bf16[128,2,1536]{2,1,0:T(2,128)(2,1)} %param.6) | copy-start | bytes 2359300
  113.1 3.0 %copy-start.1 = (bf16[768,2048]{1,0:T(8,128)(2,1)S(1)}, bf16[768,2048]{1,0:T(8,128)(2,1)}, u32[]{:S(2)}) copy-start(bf16[768,2048]{1,0:T(8,128)(2,1)} %get-tuple-element.16) | copy-start | bytes 9437188

commit v4 on v3

--- a/solution.py
+++ b/solution.py
@@ -108,7 +108,7 @@
     return (mine & (col == (row // BASE) * rest + row % rest)).astype(BF16)
 
 
-def pack_kernel(
+def pack(
     experts, rest, fold, replicas, s_fold,
     routes, rows, scaled0, scaled1,
     main, left, smain, sleft, pos,
@@ -158,9 +158,9 @@
 
 def exchange_kernel(
     experts, rest, fold, s_fold,
-    main, left, smain, sleft, w_hbm,
-    ret_out, grad_out,
-    w, x_main, x_left, z, s_main, s_left, s_rest, s_turn, s_turn_rest,
+    routes, rows_in, scaled0, scaled1, w_hbm,
+    ret_out, grad_out, pos,
+    main, left, smain, sleft, w, x_main, x_left, z, s_main, s_left, s_rest, s_turn, s_turn_rest,
     mine_f32, out_px, in_px, out_pl, in_pl, c_main, c_left, r_main, r_left,
     w_sem, tx, rx, txl, rxl, ts, rs, tsl, rsl, tp, rp, tc, rc, tcl, rcl,
 ):
@@ -222,6 +222,11 @@
         )
 
     each(devices, me, greet)
+    pack(
+        experts, rest, fold, 2, s_fold,
+        routes, rows_in, scaled0, scaled1,
+        main, left, smain, sleft, pos,
+    )
     pl.semaphore_wait(barrier, devices - 1)
 
     def start_across(k, carry):
@@ -394,29 +399,22 @@
         scaled_hidden(saved_pre[:, k], gate_weight[:, k], hidden) for k in range(2)
     ]
     vmem = pl.BlockSpec(memory_space=pltpu.VMEM)
-    *packed, positions = pl.pallas_call(
-        functools.partial(pack_kernel, experts, rest, fold, replicas, s_fold),
-        out_shape=(
-            jax.ShapeDtypeStruct((own, width), BF16),
-            jax.ShapeDtypeStruct((own, width // fold), BF16),
-            jax.ShapeDtypeStruct((own, hidden), BF16),
-            jax.ShapeDtypeStruct((own, 256), BF16),
-            jax.ShapeDtypeStruct((2, tokens), jnp.int32),
-        ),
-        in_specs=[vmem] * 4,
-        out_specs=[vmem] * 5,
-    )(routes.T, grad_out, scaled[0], scaled[1])
     dma = pltpu.SemaphoreType.DMA
     total = devices * BASE
-    back, grad_down = pl.pallas_call(
+    back, grad_down, positions = pl.pallas_call(
         functools.partial(exchange_kernel, experts, rest, fold, s_fold),
         out_shape=(
             jax.ShapeDtypeStruct((own + rest_own, hidden), BF16),
             jax.ShapeDtypeStruct((hidden, half), BF16),
+            jax.ShapeDtypeStruct((2, tokens), jnp.int32),
         ),
         in_specs=[vmem] * 4 + [pl.BlockSpec(memory_space=pl.ANY)],
-        out_specs=[vmem] * 2,
+        out_specs=[vmem] * 3,
         scratch_shapes=[
+            pltpu.VMEM((own, width), BF16),
+            pltpu.VMEM((own, width // fold), BF16),
+            pltpu.VMEM((own, hidden), BF16),
+            pltpu.VMEM((own, 256), BF16),
             pltpu.VMEM((hidden, half), BF16),
             pltpu.VMEM((total, half), BF16),
             pltpu.VMEM((total, half // fold), BF16),
@@ -442,7 +440,7 @@
             dma((experts,)), dma((experts,)), dma((experts,)), dma((experts,)),
         ],
         compiler_params=pltpu.CompilerParams(collective_id=0, has_side_effects=True),
-    )(*packed, w_down[0])
+    )(routes.T, grad_out, scaled[0], scaled[1], w_down[0])
     slot_ids = jnp.arange(own + rest_own, dtype=jnp.int32)
     pick = (positions[:, :, None] == slot_ids).astype(BF16).reshape(2 * tokens, -1)
     contraction = dot(pick, back, ((1,), (0,))).astype(BF16).reshape(2, tokens, hidden)

time: 118 us -> 116 us (0.983)
  Pallas kernels: 106 us -> 101 us
  other arithmetic: 2.93 us -> 4.33 us
    pallas_call x1 -> x0, Pallas kernels: 4.13 us -> none  [on_device(): pl.pallas_call(functools.partial(pack_kernel, experts, rest, fold, replic...]
    unnamed x10 -> x4, local copies, waits for them, and re-layouts: 3.37 us -> 3.36 us
where the time goes in v4:
time: 116 us
  Pallas kernels  101 us (87%)
  local copies, waits for them, and re-layouts  7.87 us (7%)
  other arithmetic  4.33 us (4%)
  matrix products  1.45 us (1%)
    pallas_call x1, Pallas kernels, on_device(): pl.pallas_call(functools.partial(exchange_kernel, experts, rest, fold, s_...  101 us
    unnamed x4, local copies, waits for them, and re-layouts  3.36 us
    slice x1, local copies, waits for them, and re-layouts, on_device(): saved_pre[:, k]  2.72 us

profile of v4, /device:TPU:1, one launch (start us, length us, event | category | flops | bytes accessed | tf_op | source)
XLA Modules:
  0.0 115.7 jit_solution(4287582204536751156)
XLA Ops:
  0.6 0.7 convert_element_type.49
  1.3 0.7 bitcast_convert_fusion
  2.0 1.7 %fusion.24 = (bf16[128,2,768]{2,1,0:T(2,128)(2,1)S(1)}, bf16[128,2,768]{2,1,0:T(2,128)(2,1)S(1)}) fusion(bf16[128,2,1536]{2,1,0:T(2,128)(2,1)} %param.6), kind=kLoop, calls=%fused_computation.45 | loop fusion | bytes 1572864 | tf_op jit(solution)/shard_map/slice | solution.py:23
  3.7 2.7 %fusion.25 = (bf16[128,1,1536]{2,1,0:T(2,128)(2,1)S(1)}, bf16[128,1,1536]{2,1,0:T(2,128)(2,1)S(1)}) fusion(bf16[128,2,1536]{2,1,0:T(2,128)(2,1)} %param.6), kind=kLoop, calls=%fused_computation.46 | loop fusion | bytes 1572864 | tf_op jit(solution)/shard_map/slice | solution.py:399
  6.4 0.1 copy_bitcast_fusion
  6.5 0.8 fusion.21.scaled1
  7.4 0.8 fusion.22.scaled0
  8.2 101.4 %shard_map.76 = (bf16[320,768]{1,0:T(8,128)(2,1)}, bf16[768,2048]{1,0:T(8,128)(2,1)}, s32[2,128]{1,0:T(2,128)}) custom-call(s32[2,128]{1,0:T(2,128)} %bitcast.21, bf16[128,4096]{1,0:T(8,128)(2,1)} %rows_in.1, bf16[128,768]{1,0:T(8,128)(2,1)} %fusion.22.scaled0, bf16[128,768]{1,0:T(8,128)(2,1)} %fusion.21.scaled1, bf16[768,2048]{1,0:T(8,128)(2,1)} %bitcast.19), custom_call_target="tpu_custom_call" | custom-call | tf_op jit(solution)/shard_map/pallas_call | solution.py:404
  109.6 1.4 %convolution_convert_fusion = bf16[256,768]{1,0:T(8,128)(2,1)S(1)} fusion(bf16[320,768]{1,0:T(8,128)(2,1)} %get-tuple-element.7, s32[256]{0:T(256)} %bitcast.22), kind=kOutput, calls=%fused_computation | convolution fusion | flops 126107648 | bytes 885760 | tf_op jit(solution)/shard_map/dot_general | solution.py:44
  111.0 0.0 copy-start
  111.1 1.2 %fusion.2 = (bf16[128,2]{0,1:T(2,128)(2,1)}, bf16[128,2,768]{2,0,1:T(8,128)(2,1)S(1)}, bf16[128,2,768]{2,0,1:T(8,128)(2,1)S(1)}) fusion(bf16[128,2,768]{2,1,0:T(2,128)(2,1)S(1)} %get-tuple-element.15, bf16[128,2,768]{2,1,0:T(2,128)(2,1)S(1)} %get-tuple-element.16, bf16[128,1,768]{2,0,1:T(8,128)(2,1)S(1)} %get-tuple-element.20, ...), kind=kLoop, calls=%fused_computation.10 | loop fusion | flops 4914944 | bytes 1967616 | tf_op jit(solution)/shard_map/reduce_sum | solution.py:30
  112.3 0.1 pad_maximum_fusion
  112.4 1.7 %copy.12 = bf16[128,2,1536]{2,1,0:T(2,128)(2,1)} copy(bf16[128,2,1536]{2,0,1:T(8,128)(2,1)S(1)} %pad_maximum_fusion) | data formatting | bytes 1572864
  114.1 0.0 copy-done
  114.1 1.7 %copy.28 = bf16[1,768,2048]{2,1,0:T(8,128)(2,1)} copy(bf16[1,768,2048]{2,1,0:T(8,128)(2,1)S(1)} %bitcast.20) | data formatting | bytes 6291456
  (1 shorter events, 0.0 us)
Async XLA Ops:
  111.0 3.0 %copy-start = (bf16[768,2048]{1,0:T(8,128)(2,1)S(1)}, bf16[768,2048]{1,0:T(8,128)(2,1)}, u32[]{:S(2)}) copy-start(bf16[768,2048]{1,0:T(8,128)(2,1)} %get-tuple-element.8) | copy-start | bytes 9437188
